TPU v7x, 128 devices: a whole 4x4x4 slice. The times are simulated.
128 devices in a mesh: shard: 16 (over y, z), tensor: 4 (over x), section: 2 (over core).
Axes of the slice: x: 4, y: 4, z: 4, core: 2. Of those that a mesh axis runs over, the one named last changes fastest.
Arguments:
- attention_grads: float32 [16, 4, 768, 768], P('shard', 'section', 'tensor'), may hold values from -48 to 48
- feedforward_grads: float32 [16, 2, 3072, 768], P('shard', 'section', 'tensor'), may hold values from -48 to 48
- attention_errors: float32 [16, 4, 768, 768], P('shard', 'section', 'tensor'), may hold values from -3 to 3
- feedforward_errors: float32 [16, 2, 3072, 768], P('shard', 'section', 'tensor'), may hold values from -3 to 3
- attention_factor: float32 [4, 768, 32], P('section'), may hold values from -0.21875 to 0.21875
- feedforward_factor: float32 [2, 768, 32], P('section'), may hold values from -0.21875 to 0.21875
- attention_momentum: float32 [4, 768, 768], P('section', 'tensor', 'shard'), may hold values from -3 to 3
- feedforward_momentum: float32 [2, 3072, 768], P('section', 'tensor', 'shard'), may hold values from -3 to 3
- attention_master: float32 [4, 768, 768], P('section', 'tensor', 'shard'), may hold values from -3 to 3
- feedforward_master: float32 [2, 3072, 768], P('section', 'tensor', 'shard'), may hold values from -3 to 3
- gain_grads: float32 [16, 2, 768], P('shard', 'section', 'tensor'), may hold values from -6 to 6
- bias_grads: float32 [16, 12, 32], P('shard', 'tensor'), may hold values from -6 to 6
- gain_momentum: float32 [2, 768], P('section', 'tensor'), may hold values from -3 to 3
- gain_weight: float32 [2, 768], P('section', 'tensor'), may hold values from 0.5 to 1.5
- bias_momentum: float32 [12, 32], P('tensor'), may hold values from -3 to 3
- bias_weight: float32 [12, 32], P('tensor'), may hold values from -4 to 4
Outputs:
- attention_errors_new: float32 [16, 4, 768, 768], P('shard', 'section', 'tensor')
- feedforward_errors_new: float32 [16, 2, 3072, 768], P('shard', 'section', 'tensor')
- attention_factor_new: float32 [4, 768, 32], P('section')
- feedforward_factor_new: float32 [2, 768, 32], P('section')
- attention_momentum_new: float32 [4, 768, 768], P('section', 'tensor', 'shard')
- feedforward_momentum_new: float32 [2, 3072, 768], P('section', 'tensor', 'shard')
- attention_master_new: float32 [4, 768, 768], P('section', 'tensor', 'shard')
- feedforward_master_new: float32 [2, 3072, 768], P('section', 'tensor', 'shard')
- attention_fresh: bfloat16 [4, 768, 768], P('section', 'tensor')
- feedforward_fresh: bfloat16 [2, 3072, 768], P('section', 'tensor')
- gain_momentum_new: float32 [2, 768], P('section', 'tensor')
- gain_weight_new: float32 [2, 768], P('section', 'tensor')
- bias_momentum_new: float32 [12, 32], P('tensor')
- bias_weight_new: float32 [12, 32], P('tensor')
All inputs are finite; a program needn't handle non-finite values.
Results may differ from a plain program's by a relative error of at most 0.0004.
Values may be sent and summed in bfloat16 or wider, within the bound.
A program may use at most 64 MiB of HBM per device.

v0:
```python
import jax
import jax.numpy as jnp
from jax import lax
from jax.sharding import PartitionSpec as P

NS_STEPS = 5
exact_mode = lax.Precision.HIGHEST
learn_rate = 0.05
decay_rate = 0.9


def inverse_root(gram_matrix):
    identity = jnp.broadcast_to(
        jnp.eye(gram_matrix.shape[-1], dtype=jnp.float32), gram_matrix.shape
    )
    frob_scale = jnp.sqrt(jnp.sum(gram_matrix * gram_matrix, axis=(-2, -1), keepdims=True)) + 1e-06
    converge = gram_matrix / frob_scale
    inverse = identity
    for turn_index in range(NS_STEPS):
        middle = 0.5 * (3.0 * identity - jnp.matmul(inverse, converge, precision=exact_mode))
        converge, inverse = (
            jnp.matmul(converge, middle, precision=exact_mode),
            jnp.matmul(middle, inverse, precision=exact_mode),
        )
    return inverse / jnp.sqrt(frob_scale)


def left_terms(merged, factor):
    return jnp.einsum("rmij,mjk->mik", merged, factor, precision=exact_mode)


def row_gram(matrix):
    return jnp.einsum("mik,mil->mkl", matrix, matrix, precision=exact_mode)


def right_terms(merged, ortho):
    return jnp.einsum("rmij,mik->mjk", merged, ortho, precision=exact_mode)


def per_device(
    attention_grads,
    feedforward_grads,
    attention_errors,
    feedforward_errors,
    attention_factor,
    feedforward_factor,
    attention_momentum,
    feedforward_momentum,
    attention_master,
    feedforward_master,
    gain_grads,
    bias_grads,
    gain_momentum,
    gain_weight,
    bias_momentum,
    bias_weight,
):
    replicas = lax.axis_size("shard")
    column_width = attention_master.shape[2]
    column_start = lax.axis_index("shard") * column_width
    attention_base = attention_master - learn_rate * decay_rate * attention_momentum
    feedforward_base = feedforward_master - learn_rate * decay_rate * feedforward_momentum
    attention_merged = attention_grads + attention_errors
    feedforward_merged = feedforward_grads + feedforward_errors
    attention_part = left_terms(attention_merged, attention_factor)
    feedforward_part = left_terms(feedforward_merged, feedforward_factor)
    attention_power, feedforward_power = lax.psum((attention_part, feedforward_part), "shard")
    attention_gram, feedforward_gram = lax.psum(
        (row_gram(attention_power), row_gram(feedforward_power)), "tensor"
    )
    attention_ortho = jnp.matmul(
        attention_power, inverse_root(attention_gram), precision=exact_mode
    )
    feedforward_ortho = jnp.matmul(
        feedforward_power, inverse_root(feedforward_gram), precision=exact_mode
    )
    attention_back, feedforward_back = lax.psum(
        (
            right_terms(attention_merged, attention_ortho),
            right_terms(feedforward_merged, feedforward_ortho),
        ),
        ("shard", "tensor"),
    )
    attention_back = attention_back / replicas
    feedforward_back = feedforward_back / replicas
    attention_approx = jnp.einsum(
        "mik,mjk->mij", attention_ortho, attention_back, precision=exact_mode
    )
    feedforward_approx = jnp.einsum(
        "mik,mjk->mij", feedforward_ortho, feedforward_back, precision=exact_mode
    )
    attention_errors_new = attention_merged - attention_approx[None]
    feedforward_errors_new = feedforward_merged - feedforward_approx[None]
    attention_factor_new = jnp.matmul(
        attention_back, inverse_root(row_gram(attention_back)), precision=exact_mode
    )
    feedforward_factor_new = jnp.matmul(
        feedforward_back, inverse_root(row_gram(feedforward_back)), precision=exact_mode
    )
    attention_slice = lax.dynamic_slice_in_dim(attention_approx, column_start, column_width, 2)
    feedforward_slice = lax.dynamic_slice_in_dim(feedforward_approx, column_start, column_width, 2)
    attention_momentum_new = decay_rate * attention_momentum + attention_slice
    feedforward_momentum_new = decay_rate * feedforward_momentum + feedforward_slice
    attention_master_new = attention_base - learn_rate * attention_slice
    feedforward_master_new = feedforward_base - learn_rate * feedforward_slice
    attention_fresh, feedforward_fresh = (
        lax.all_gather(attention_master_new.astype(jnp.bfloat16), "shard", axis=2, tiled=True),
        lax.all_gather(feedforward_master_new.astype(jnp.bfloat16), "shard", axis=2, tiled=True),
    )
    gain_total, bias_total = lax.psum((gain_grads[0], bias_grads[0]), "shard")
    gain_momentum_new = decay_rate * gain_momentum + gain_total / replicas
    gain_weight_new = gain_weight - learn_rate * gain_momentum_new
    bias_momentum_new = decay_rate * bias_momentum + bias_total / replicas
    bias_weight_new = bias_weight - learn_rate * bias_momentum_new
    return (
        attention_errors_new,
        feedforward_errors_new,
        attention_factor_new,
        feedforward_factor_new,
        attention_momentum_new,
        feedforward_momentum_new,
        attention_master_new,
        feedforward_master_new,
        attention_fresh,
        feedforward_fresh,
        gain_momentum_new,
        gain_weight_new,
        bias_momentum_new,
        bias_weight_new,
    )


def solution(mesh):
    placed = (
        P("shard", "section", "tensor", None),
        P("shard", "section", "tensor", None),
        P("shard", "section", "tensor", None),
        P("shard", "section", "tensor", None),
        P("section", None, None),
        P("section", None, None),
        P("section", "tensor", "shard"),
        P("section", "tensor", "shard"),
        P("section", "tensor", "shard"),
        P("section", "tensor", "shard"),
        P("shard", "section", "tensor"),
        P("shard", "tensor", None),
        P("section", "tensor"),
        P("section", "tensor"),
        P("tensor", None),
        P("tensor", None),
    )
    return jax.shard_map(
        per_device,
        mesh=mesh,
        in_specs=placed,
        out_specs=(
            P("shard", "section", "tensor", None),
            P("shard", "section", "tensor", None),
            P("section", None, None),
            P("section", None, None),
            P("section", "tensor", "shard"),
            P("section", "tensor", "shard"),
            P("section", "tensor", "shard"),
            P("section", "tensor", "shard"),
            P("section", "tensor", None),
            P("section", "tensor", None),
            P("section", "tensor"),
            P("section", "tensor"),
            P("tensor", None),
            P("tensor", None),
        ),
        check_vma=False,
    )
```

profile of v0, /device:TPU:0, one launch (start us, length us, event | category | flops | bytes accessed | tf_op | source)
XLA Modules:
  0.0 321.8 jit_solution(5114528691584657770)
XLA Ops:
  7.3 3.2 copy.39
  10.5 2.0 copy.40
  12.4 2.7 add.70
  15.1 2.2 fusion.2
  17.4 1.8 add.68
  21.5 76.9 %all-reduce.1 = (f32[2,192,32]{1,2,0:T(8,128)S(1)}, f32[1,192]{1,0:T(1,128)S(1)}, f32[3,32]{1,0:T(4,128)S(1)}) all-reduce(f32[2,192,32]{1,2,0:T(8,128)S(1)} %fusion.6, f32[1,192]{1,0:T(1,128)S(1)} %bitcast.162, f32[3,32]{1,0:T(4,128)S(1)} %bitcast.161), channel_id=1, replica_groups=mesh['shard'=16,'tensor'=4,'section'=2] {'shard'}, use_global_device_ids=true, to_apply=%region_0.0 | all-reduce | flops 12576 | bytes 100608 | tf_op jit(solution)/shard_map/psum | solution.py:67
  98.6 3.7 %all-reduce.6.cloned.1.call-done = f32[768,32]{0,1:T(8,128)} async-done(((f32[768,32]{0,1:T(8,128)}), f32[768,32]{0,1:T(8,128)}) %all-reduce.6.cloned.1.call-update) | async-done | bytes 98320 | tf_op jit(solution)/shard_map/psum | solution.py:67
  103.6 17.4 %all-reduce.2 = (f32[2,32,32]{2,1,0:T(8,128)S(1)}, f32[1,32,32]{2,1,0:T(8,128)S(1)}) all-reduce(f32[2,32,32]{2,1,0:T(8,128)S(1)} %fusion.78, f32[1,32,32]{2,1,0:T(8,128)S(1)} %convolution_bitcast_fusion.1), channel_id=1, replica_groups=mesh['shard'=16,'tensor'=4,'section'=2] {'tensor'}, use_global_device_ids=true, to_apply=%region_1.0 | all-reduce | flops 3072 | bytes 24576 | tf_op jit(solution)/shard_map/psum | solution.py:68
  127.1 2.8 fusion.8
  130.5 1.4 fusion.4
  133.7 121.8 %all-reduce.8.cloned.1.call-done = (f32[2,768,32]{1,2,0:T(8,128)}, f32[1,768,32]{1,2,0:T(8,128)}) async-done(((f32[2,768,32]{1,2,0:T(8,128)}, f32[1,768,32]{1,2,0:T(8,128)}), (f32[2,768,32]{1,2,0:T(8,128)}, f32[1,768,32]{1,2,0:T(8,128)})) %all-reduce.8.cloned.1.call-update) | async-done | bytes 294928 | tf_op jit(solution)/shard_map/psum | solution.py:77
  255.5 1.8 multiply_reduce_fusion.2
  259.8 1.4 multiply_reduce_fusion
  264.2 4.5 %bitcast_subtract_fusion = (f32[1,1,768,768]{2,3,1,0:T(8,128)}, f32[768,768]{0,1:T(8,128)S(1)}) fusion(f32[1,1,768,768]{2,3,1,0:T(8,128)S(1)} %add.70, f32[768,32]{0,1:T(8,128)S(1)} %fusion.92, f32[1,768,32]{1,2,0:T(8,128)} %get-tuple-element.43), kind=kOutput, calls=%fused_computation | convolution fusion | flops 227106816 | bytes 7274496 | tf_op jit(solution)/shard_map/mik,mjk->mij/dot_general | solution.py:89
  268.7 2.6 bitcast_subtract_fusion.1
  272.1 1.9 fusion.77
  275.6 22.5 %all_gather.6 = bf16[2,192,768]{1,0,2:T(2,128)(2,1)S(1)} all-gather(bf16[2,192,48]{1,0,2:T(2,128)(2,1)} %copy.44), channel_id=1, replica_groups=mesh['shard'=16,'tensor'=4,'section'=2] {'shard'}, dimensions={2}, use_global_device_ids=true | all-gather | bytes 626688 | tf_op jit(solution)/shard_map/all_gather | solution.py:107
  298.2 2.0 copy.45
  300.1 1.7 copy.48
  301.8 1.7 copy.46
  303.5 1.7 copy.47
  305.2 1.8 convolution_bitcast_fusion
  311.0 1.9 all-gather.2.cloned.1.call-done
  312.9 2.4 copy.49
  (123 shorter events, 22.3 us)
Async XLA Ops:
  7.2 13.0 %copy-start = (f32[2,768,32]{1,2,0:T(8,128)S(1)}, f32[2,768,32]{1,2,0:T(8,128)}, u32[]{:S(2)}) copy-start(f32[2,768,32]{1,2,0:T(8,128)} %param.20) | copy-start | bytes 589828
  7.2 3.3 %copy-start.5 = (f32[1,1,768,768]{3,2,1,0:T(8,128)S(1)}, f32[1,1,768,768]{3,2,1,0:T(8,128)}, u32[]{:S(2)}) copy-start(f32[1,1,768,768]{3,2,1,0:T(8,128)} %param.19) | copy-start | bytes 7077892
  7.2 95.1 %all-reduce.6.cloned.1.call-start = ((), (), s32[]{:S(2)}) async-start(), calls=%async_computation | async-start | bytes 196608 | tf_op jit(solution)/shard_map/psum | solution.py:67
  12.4 2.7 copy-start.11
  15.1 2.3 copy-start.16
  17.3 238.1 %all-reduce.8.cloned.1.call-start = ((), (), s32[]{:S(2)}) async-start(), calls=%async_computation.2 | async-start | bytes 589824 | tf_op jit(solution)/shard_map/psum | solution.py:77
  17.4 4.0 %copy-start.17 = (f32[1,1,192]{2,1,0:T(1,128)S(1)}, f32[1,1,192]{2,1,0:T(1,128)}, u32[]{:S(2)}) copy-start(f32[1,1,192]{2,1,0:T(1,128)} %param.26) | copy-start | bytes 2308
  19.2 1.0 copy-start.1
  102.3 24.4 %copy-start.7 = (f32[768,32]{0,1:T(8,128)S(1)}, f32[768,32]{0,1:T(8,128)}, u32[]{:S(2)}) copy-start(f32[768,32]{0,1:T(8,128)} %all-reduce.6.cloned.1.call-done) | copy-start | bytes 294916
  124.1 6.4 %copy-start.2 = (f32[1,2,192,768]{3,2,1,0:T(8,128)S(1)}, f32[1,2,192,768]{3,2,1,0:T(8,128)}, u32[]{:S(2)}) copy-start(f32[1,2,192,768]{3,2,1,0:T(8,128)} %copy-done.1) | copy-start | bytes 3538948
  127.0 5.2 %copy-start.18 = (f32[1,192]{1,0:T(1,128)S(1)}, f32[1,192]{1,0:T(1,128)}, u32[]{:S(2)}) copy-start(f32[1,192]{1,0:T(1,128)} %param.29) | copy-start | bytes 2308
  127.0 5.2 %copy-start.19 = (f32[1,192]{1,0:T(1,128)S(1)}, f32[1,192]{1,0:T(1,128)}, u32[]{:S(2)}) copy-start(f32[1,192]{1,0:T(1,128)} %param.28) | copy-start | bytes 2308
  127.0 5.8 %copy-start.12 = (f32[2,192,48]{1,2,0:T(8,128)S(1)}, f32[2,192,48]{1,2,0:T(8,128)}, u32[]{:S(2)}) copy-start(f32[2,192,48]{1,2,0:T(8,128)} %param.22) | copy-start | bytes 221188
  127.0 5.9 %copy-start.13 = (f32[2,192,48]{1,2,0:T(8,128)S(1)}, f32[2,192,48]{1,2,0:T(8,128)}, u32[]{:S(2)}) copy-start(f32[2,192,48]{1,2,0:T(8,128)} %param.24) | copy-start | bytes 221188
  127.0 6.0 %copy-start.14 = (f32[3,32]{1,0:T(4,128)S(1)}, f32[3,32]{1,0:T(4,128)}, u32[]{:S(2)}) copy-start(f32[3,32]{1,0:T(4,128)} %param.31) | copy-start | bytes 1156
  127.1 6.0 %copy-start.15 = (f32[3,32]{1,0:T(4,128)S(1)}, f32[3,32]{1,0:T(4,128)}, u32[]{:S(2)}) copy-start(f32[3,32]{1,0:T(4,128)} %param.30) | copy-start | bytes 1156
  132.0 181.0 %all-gather.2.cloned.1.call-start = ((), (), s32[]{:S(2)}) async-start(), calls=%async_computation.1 | async-start | bytes 1253376 | tf_op jit(solution)/shard_map/all_gather | solution.py:108
  264.2 4.5 %copy-start.3 = (f32[1,2,192,768]{3,2,1,0:T(8,128)S(1)}, f32[1,2,192,768]{3,2,1,0:T(8,128)}, u32[]{:S(2)}) copy-start(f32[1,2,192,768]{3,2,1,0:T(8,128)} %copy-done.1) | copy-start | bytes 3538948
  264.2 4.5 %copy-start.6 = (f32[2,768,32]{1,2,0:T(8,128)S(1)}, f32[2,768,32]{1,2,0:T(8,128)}, u32[]{:S(2)}) copy-start(f32[2,768,32]{1,2,0:T(8,128)} %get-tuple-element.42) | copy-start | bytes 589828
  268.7 2.6 copy-start.9
  268.7 2.6 copy-start.10
  271.3 26.9 %copy-start.4 = (f32[1,1,768,768]{2,3,1,0:T(8,128)S(1)}, f32[1,1,768,768]{2,3,1,0:T(8,128)}, u32[]{:S(2)}) copy-start(f32[1,1,768,768]{2,3,1,0:T(8,128)} %get-tuple-element.65) | copy-start | bytes 7077892
  300.1 8.8 %copy-start.8 = (f32[2,32,32]{2,1,0:T(8,128)S(1)}, f32[2,32,32]{2,1,0:T(8,128)}, u32[]{:S(2)}) copy-start(f32[2,32,32]{2,1,0:T(8,128)} %fusion.93) | copy-start | bytes 24580
  300.1 9.6 %copy-start.20 = (f32[2]{0:T(128)S(1)}, f32[2]{0:T(128)}, u32[]{:S(2)}) copy-start(f32[2]{0:T(128)} %get-tuple-element.59) | copy-start | bytes 28
Sparse Core Ops, SparseCore 0:
  17.5 84.7 all-reduce.5
  132.1 123.3 all-reduce.7
  272.2 40.6 all-gather.1
where the time goes:
time: 322 us
  waiting for transfers between devices  128 us (40%)
  blocking collectives  117 us (36%)
  matrix products  35.2 us (11%)
  local copies, waits for them, and re-layouts  16.6 us (5%)
  between operations  15.8 us (5%)
  other arithmetic  9.61 us (3%)
    psum x1, waiting for transfers between devices, per_device(): lax.psum((right_terms(attention_merged, attention_ortho), right_terms(fee...  122 us
    psum x1, blocking collectives, per_device(): lax.psum((attention_part, feedforward_part), 'shard')  76.9 us
    all_gather x1, blocking collectives, per_device(): lax.all_gather(attention_master_new.astype(jnp.bfloat16), 'shard', axis=2...  22.5 us
    psum x1, blocking collectives, per_device(): lax.psum((row_gram(attention_power), row_gram(feedforward_power)), 'tensor')  17.4 us
    unnamed x52, local copies, waits for them, and re-layouts  15.9 us
  transfers between devices with their start and end apart: 3, of which 3 were waited for; matrix products, arithmetic and copies ran while one was open for 6% of the time, Pallas kernels for 0%

commit v1 on v0

--- a/solution.py
+++ b/solution.py
@@ -7,6 +7,19 @@
 exact_mode = lax.Precision.HIGHEST
 learn_rate = 0.05
 decay_rate = 0.9
+
+
+def collect(value, axis, dim):
+    ways = lax.axis_size(axis)
+    up = [(d, (d + 1) % ways) for d in range(ways)]
+    down = [(d, (d - 1) % ways) for d in range(ways)]
+    earlier, later = ([value], [value])
+    for _ in range(ways // 2):
+        earlier.append(lax.ppermute(earlier[-1], axis, up))
+    for _ in range((ways - 1) // 2):
+        later.append(lax.ppermute(later[-1], axis, down))
+    line = jnp.concatenate([*earlier[::-1], *later[1:]], axis=dim)
+    return jnp.roll(line, (lax.axis_index(axis) - ways // 2) * value.shape[dim], axis=dim)
 
 
 def inverse_root(gram_matrix):
@@ -104,7 +117,7 @@
     attention_master_new = attention_base - learn_rate * attention_slice
     feedforward_master_new = feedforward_base - learn_rate * feedforward_slice
     attention_fresh, feedforward_fresh = (
-        lax.all_gather(attention_master_new.astype(jnp.bfloat16), "shard", axis=2, tiled=True),
+        collect(attention_master_new.astype(jnp.bfloat16), "shard", 2),
         lax.all_gather(feedforward_master_new.astype(jnp.bfloat16), "shard", axis=2, tiled=True),
     )
     gain_total, bias_total = lax.psum((gain_grads[0], bias_grads[0]), "shard")

time: 322 us -> 355 us (1.10)
  starting transfers between devices: 0.3 us -> 35.4 us
  blocking collectives: 117 us -> 94.2 us
  waiting for transfers between devices: 128 us -> 146 us
  local copies, waits for them, and re-layouts: 16.6 us -> 20.4 us
    ppermute x0 -> x15, starting transfers between devices: none -> 35.3 us  [the longest x7 35.2 us: collect(): later.append(lax.ppermute(later[-1], axis, down))]
    all_gather x1 -> x0, blocking collectives: 22.5 us -> none  [per_device(): lax.all_gather(attention_master_new.astype(jnp.bfloat16), 'shard', axis=2...]
    ppermute x0 -> x15, waiting for transfers between devices: none -> 21.1 us  [the longest x8 21 us: collect(): earlier.append(lax.ppermute(earlier[-1], axis, up))]
    concatenate x0 -> x1, local copies, waits for them, and re-layouts: none -> 5.09 us  [collect(): jnp.roll(line, (lax.axis_index(axis) - ways // 2) * value.shape[dim], axi...]
    unnamed x52 -> x67, local copies, waits for them, and re-layouts: 15.9 us -> 14.2 us
  transfers between devices with their start and end apart: 3 -> 18, of which waited for: 3 -> 10; matrix products, arithmetic and copies ran while one was open for 6% -> 7% of each run, Pallas kernels for 0% -> 0%
where the time goes in v1:
time: 355 us; the launch traced here: 354 us
  waiting for transfers between devices  146 us (41%)
  blocking collectives  94.2 us (27%)
  starting transfers between devices  35.4 us (10%)
  matrix products  34.9 us (10%)
  local copies, waits for them, and re-layouts  20.4 us (6%)
  between operations  15.8 us (4%)
  other arithmetic  7.82 us (2%)
    psum x1, waiting for transfers between devices, per_device(): lax.psum((right_terms(attention_merged, attention_ortho), right_terms(fee...  121 us
    psum x1, blocking collectives, per_device(): lax.psum((attention_part, feedforward_part), 'shard')  76.9 us
    ppermute x7, starting transfers between devices, collect(): later.append(lax.ppermute(later[-1], axis, down))  35.2 us
    ppermute x8, waiting for transfers between devices, collect(): earlier.append(lax.ppermute(earlier[-1], axis, up))  21 us
    psum x1, blocking collectives, per_device(): lax.psum((row_gram(attention_power), row_gram(feedforward_power)), 'tensor')  17.3 us
    unnamed x67, local copies, waits for them, and re-layouts  14.2 us
  transfers between devices with their start and end apart: 18, of which 10 were waited for; matrix products, arithmetic and copies ran while one was open for 7% of the time, Pallas kernels for 0%

profile of v1, /device:TPU:0, one launch (start us, length us, event | category | flops | bytes accessed | tf_op | source)
XLA Modules:
  0.0 354.1 jit_solution(261750418369688521)
XLA Ops:
  7.3 3.2 copy.30
  12.4 2.7 add.81
  15.2 2.2 fusion.2
  21.5 76.9 %all-reduce.1 = (f32[2,192,32]{1,2,0:T(8,128)S(1)}, f32[1,192]{1,0:T(1,128)S(1)}, f32[3,32]{1,0:T(4,128)S(1)}) all-reduce(f32[2,192,32]{1,2,0:T(8,128)S(1)} %fusion.6, f32[1,192]{1,0:T(1,128)S(1)} %bitcast.162, f32[3,32]{1,0:T(4,128)S(1)} %bitcast.161), channel_id=1, replica_groups=mesh['shard'=16,'tensor'=4,'section'=2] {'shard'}, use_global_device_ids=true, to_apply=%region_0.0 | all-reduce | flops 12576 | bytes 100608 | tf_op jit(solution)/shard_map/psum | solution.py:80
  98.6 3.7 %all-reduce.6.cloned.1.call-done = f32[768,32]{0,1:T(8,128)} async-done(((f32[768,32]{0,1:T(8,128)}), f32[768,32]{0,1:T(8,128)}) %all-reduce.6.cloned.1.call-update) | async-done | bytes 98320 | tf_op jit(solution)/shard_map/psum | solution.py:80
  103.5 17.3 %all-reduce.2 = (f32[2,32,32]{2,1,0:T(8,128)S(1)}, f32[1,32,32]{2,1,0:T(8,128)S(1)}) all-reduce(f32[2,32,32]{2,1,0:T(8,128)S(1)} %fusion.78, f32[1,32,32]{2,1,0:T(8,128)S(1)} %convolution_bitcast_fusion.1), channel_id=1, replica_groups=mesh['shard'=16,'tensor'=4,'section'=2] {'tensor'}, use_global_device_ids=true, to_apply=%region_1.0 | all-reduce | flops 3072 | bytes 24576 | tf_op jit(solution)/shard_map/psum | solution.py:81
  127.5 2.8 fusion.8
  134.7 120.6 %all-reduce.8.cloned.1.call-done = (f32[2,768,32]{1,2,0:T(8,128)}, f32[1,768,32]{1,2,0:T(8,128)}) async-done(((f32[2,768,32]{1,2,0:T(8,128)}, f32[1,768,32]{1,2,0:T(8,128)}), (f32[2,768,32]{1,2,0:T(8,128)}, f32[1,768,32]{1,2,0:T(8,128)})) %all-reduce.8.cloned.1.call-update) | async-done | bytes 294928 | tf_op jit(solution)/shard_map/psum | solution.py:90
  267.6 2.8 collective-permute-start.8
  270.4 3.5 bitcast_subtract_fusion
  279.0 5.4 %collective-permute-start.9 = (bf16[2,192,48]{2,1,0:T(8,128)(2,1)S(1)}, bf16[2,192,48]{2,1,0:T(8,128)(2,1)S(1)}, u32[]{:S(2)}, u32[]{:S(2)}) collective-permute-start(bf16[2,192,48]{2,1,0:T(8,128)(2,1)S(1)} %collective-permute-done.8), channel_id=1, source_target_pairs={{0,120},{8,0},{16,8},{24,16},{32,24},{40,32},{48,40},{56,48},{64,5... | collective-permute-start | bytes 110600 | tf_op jit(solution)/shard_map/ppermute | solution.py:20
  284.4 2.6 collective-permute-done.1
  287.2 5.4 %collective-permute-start.10 = (bf16[2,192,48]{2,1,0:T(8,128)(2,1)S(1)}, bf16[2,192,48]{2,1,0:T(8,128)(2,1)S(1)}, u32[]{:S(2)}, u32[]{:S(2)}) collective-permute-start(bf16[2,192,48]{2,1,0:T(8,128)(2,1)S(1)} %collective-permute-done.9), channel_id=1, source_target_pairs={{0,120},{8,0},{16,8},{24,16},{32,24},{40,32},{48,40},{56,48},{64,5... | collective-permute-start | bytes 110600 | tf_op jit(solution)/shard_map/ppermute | solution.py:20
  292.6 2.6 collective-permute-done.2
  295.3 5.4 %collective-permute-start.11 = (bf16[2,192,48]{2,1,0:T(8,128)(2,1)S(1)}, bf16[2,192,48]{2,1,0:T(8,128)(2,1)}, u32[]{:S(2)}, u32[]{:S(2)}) collective-permute-start(bf16[2,192,48]{2,1,0:T(8,128)(2,1)S(1)} %collective-permute-done.10), channel_id=1, source_target_pairs={{0,120},{8,0},{16,8},{24,16},{32,24},{40,32},{48,40},{56,48},{64,5... | collective-permute-start | bytes 110600 | tf_op jit(solution)/shard_map/ppermute | solution.py:20
  300.7 2.4 collective-permute-done.3
  303.8 5.0 %collective-permute-start.12 = (bf16[2,192,48]{2,1,0:T(8,128)(2,1)}, bf16[2,192,48]{2,1,0:T(8,128)(2,1)}, u32[]{:S(2)}, u32[]{:S(2)}) collective-permute-start(bf16[2,192,48]{2,1,0:T(8,128)(2,1)} %collective-permute-done.11), channel_id=1, source_target_pairs={{0,120},{8,0},{16,8},{24,16},{32,24},{40,32},{48,40},{56,48},{64,5... | collective-permute-start | bytes 110600 | tf_op jit(solution)/shard_map/ppermute | solution.py:20
  308.8 4.4 %collective-permute-done.4 = bf16[2,192,48]{2,1,0:T(8,128)(2,1)} collective-permute-done((bf16[2,192,48]{2,1,0:T(8,128)(2,1)S(1)}, bf16[2,192,48]{2,1,0:T(8,128)(2,1)}, u32[]{:S(2)}, u32[]{:S(2)}) %collective-permute-start.4) | collective-permute-done | bytes 36896 | tf_op jit(solution)/shard_map/ppermute | solution.py:18
  313.5 5.8 %collective-permute-start.13 = (bf16[2,192,48]{2,1,0:T(8,128)(2,1)}, bf16[2,192,48]{2,1,0:T(8,128)(2,1)}, u32[]{:S(2)}, u32[]{:S(2)}) collective-permute-start(bf16[2,192,48]{2,1,0:T(8,128)(2,1)} %collective-permute-done.12), channel_id=1, source_target_pairs={{0,120},{8,0},{16,8},{24,16},{32,24},{40,32},{48,40},{56,48},{64,5... | collective-permute-start | bytes 110600 | tf_op jit(solution)/shard_map/ppermute | solution.py:20
  319.3 3.2 collective-permute-done.5
  323.4 5.4 %collective-permute-start.14 = (bf16[2,192,48]{2,1,0:T(8,128)(2,1)}, bf16[2,192,48]{2,1,0:T(8,128)(2,1)}, u32[]{:S(2)}, u32[]{:S(2)}) collective-permute-start(bf16[2,192,48]{2,1,0:T(8,128)(2,1)} %collective-permute-done.13), channel_id=1, source_target_pairs={{0,120},{8,0},{16,8},{24,16},{32,24},{40,32},{48,40},{56,48},{64,5... | collective-permute-start | bytes 110600 | tf_op jit(solution)/shard_map/ppermute | solution.py:20
  335.1 3.9 %collective-permute-done.7 = bf16[2,192,48]{2,1,0:T(8,128)(2,1)} collective-permute-done((bf16[2,192,48]{2,1,0:T(8,128)(2,1)}, bf16[2,192,48]{2,1,0:T(8,128)(2,1)}, u32[]{:S(2)}, u32[]{:S(2)}) %collective-permute-start.7) | collective-permute-done | bytes 36896 | tf_op jit(solution)/shard_map/ppermute | solution.py:18
  339.0 5.1 %concatenate.6 = bf16[2,192,1536]{2,1,0:T(8,128)(2,1)S(1)} concatenate(bf16[2,192,48]{2,1,0:T(8,128)(2,1)} %collective-permute-done.7, bf16[2,192,48]{2,1,0:T(8,128)(2,1)} %collective-permute-done.6, bf16[2,192,48]{2,1,0:T(8,128)(2,1)} %collective-permute-done.5, bf16[2,192,48]{2,1,0:T(8,128)(2,1)} %collective-permute-done.4, bf16[2,192,48]{2,1,0:T(8,128)(2,1)S(1)} %copy-done.14, ...), dimensions={2} | concatenate | bytes 2359296 | tf_op jit(solution)/shard_map/jit(_roll_dynamic)/concatenate | solution.py:22
  345.2 2.4 copy.38
  (168 shorter events, 43.6 us)
Async XLA Ops:
  7.2 13.0 %copy-start = (f32[2,768,32]{1,2,0:T(8,128)S(1)}, f32[2,768,32]{1,2,0:T(8,128)}, u32[]{:S(2)}) copy-start(f32[2,768,32]{1,2,0:T(8,128)} %param.20) | copy-start | bytes 589828
  7.2 95.1 %all-reduce.6.cloned.1.call-start = ((), (), s32[]{:S(2)}) async-start(), calls=%async_computation | async-start | bytes 196608 | tf_op jit(solution)/shard_map/psum | solution.py:80
  17.4 238.0 %all-reduce.8.cloned.1.call-start = ((), (), s32[]{:S(2)}) async-start(), calls=%async_computation.2 | async-start | bytes 589824 | tf_op jit(solution)/shard_map/psum | solution.py:90
  131.9 213.3 %all-gather.2.cloned.1.call-start = ((), (), s32[]{:S(2)}) async-start(), calls=%async_computation.1 | async-start | bytes 1253376 | tf_op jit(solution)/shard_map/all_gather | solution.py:121
  255.3 10.0 %copy-start.6 = (f32[2,768,32]{1,2,0:T(8,128)S(1)}, f32[2,768,32]{1,2,0:T(8,128)}, u32[]{:S(2)}) copy-start(f32[2,768,32]{1,2,0:T(8,128)} %get-tuple-element.28) | copy-start | bytes 589828
  257.8 7.5 %copy-start.3 = (f32[1,2,192,768]{3,2,1,0:T(8,128)S(1)}, f32[1,2,192,768]{3,2,1,0:T(8,128)}, u32[]{:S(2)}) copy-start(f32[1,2,192,768]{3,2,1,0:T(8,128)} %copy-done.1) | copy-start | bytes 3538948
  267.6 11.4 %collective-permute-start.8 = (bf16[2,192,48]{2,1,0:T(8,128)(2,1)S(1)}, bf16[2,192,48]{2,1,0:T(8,128)(2,1)S(1)}, u32[]{:S(2)}, u32[]{:S(2)}) collective-permute-start(bf16[2,192,48]{2,1,0:T(8,128)(2,1)S(1)} %get-tuple-element.41), channel_id=1, source_target_pairs={{0,120},{8,0},{16,8},{24,16},{32,24},{40,32},{48,40},{56,48},{64,5... | collective-permute-start | bytes 110600 | tf_op jit(solution)/shard_map/ppermute | solution.py:20
  270.4 8.4 %collective-permute-start = (bf16[2,192,48]{2,1,0:T(8,128)(2,1)S(1)}, bf16[2,192,48]{2,1,0:T(8,128)(2,1)}, u32[]{:S(2)}, u32[]{:S(2)}) collective-permute-start(bf16[2,192,48]{2,1,0:T(8,128)(2,1)S(1)} %get-tuple-element.41), channel_id=1, source_target_pairs={{0,8},{8,16},{16,24},{24,32},{32,40},{40,48},{48,56},{56,64},{64,7... | collective-permute-start | bytes 110600 | tf_op jit(solution)/shard_map/ppermute | solution.py:18
  273.9 59.2 %copy-start.4 = (f32[1,1,768,768]{2,3,1,0:T(8,128)S(1)}, f32[1,1,768,768]{2,3,1,0:T(8,128)}, u32[]{:S(2)}) copy-start(f32[1,1,768,768]{2,3,1,0:T(8,128)} %get-tuple-element.51) | copy-start | bytes 7077892
  278.8 8.2 %collective-permute-start.1 = (bf16[2,192,48]{2,1,0:T(8,128)(2,1)}, bf16[2,192,48]{2,1,0:T(8,128)(2,1)S(1)}, u32[]{:S(2)}, u32[]{:S(2)}) collective-permute-start(bf16[2,192,48]{2,1,0:T(8,128)(2,1)} %collective-permute-done), channel_id=1, source_target_pairs={{0,8},{8,16},{16,24},{24,32},{32,40},{40,48},{48,56},{56,64},{64,7... | collective-permute-start | bytes 110600 | tf_op jit(solution)/shard_map/ppermute | solution.py:18
  279.0 8.1 %collective-permute-start.9 = (bf16[2,192,48]{2,1,0:T(8,128)(2,1)S(1)}, bf16[2,192,48]{2,1,0:T(8,128)(2,1)S(1)}, u32[]{:S(2)}, u32[]{:S(2)}) collective-permute-start(bf16[2,192,48]{2,1,0:T(8,128)(2,1)S(1)} %collective-permute-done.8), channel_id=1, source_target_pairs={{0,120},{8,0},{16,8},{24,16},{32,24},{40,32},{48,40},{56,48},{64,5... | collective-permute-start | bytes 110600 | tf_op jit(solution)/shard_map/ppermute | solution.py:20
  287.0 8.1 %collective-permute-start.2 = (bf16[2,192,48]{2,1,0:T(8,128)(2,1)S(1)}, bf16[2,192,48]{2,1,0:T(8,128)(2,1)S(1)}, u32[]{:S(2)}, u32[]{:S(2)}) collective-permute-start(bf16[2,192,48]{2,1,0:T(8,128)(2,1)S(1)} %collective-permute-done.1), channel_id=1, source_target_pairs={{0,8},{8,16},{16,24},{24,32},{32,40},{40,48},{48,56},{56,64},{64,7... | collective-permute-start | bytes 110600 | tf_op jit(solution)/shard_map/ppermute | solution.py:18
  287.2 8.1 %collective-permute-start.10 = (bf16[2,192,48]{2,1,0:T(8,128)(2,1)S(1)}, bf16[2,192,48]{2,1,0:T(8,128)(2,1)S(1)}, u32[]{:S(2)}, u32[]{:S(2)}) collective-permute-start(bf16[2,192,48]{2,1,0:T(8,128)(2,1)S(1)} %collective-permute-done.9), channel_id=1, source_target_pairs={{0,120},{8,0},{16,8},{24,16},{32,24},{40,32},{48,40},{56,48},{64,5... | collective-permute-start | bytes 110600 | tf_op jit(solution)/shard_map/ppermute | solution.py:20
  295.1 8.0 %collective-permute-start.3 = (bf16[2,192,48]{2,1,0:T(8,128)(2,1)S(1)}, bf16[2,192,48]{2,1,0:T(8,128)(2,1)S(1)}, u32[]{:S(2)}, u32[]{:S(2)}) collective-permute-start(bf16[2,192,48]{2,1,0:T(8,128)(2,1)S(1)} %collective-permute-done.2), channel_id=1, source_target_pairs={{0,8},{8,16},{16,24},{24,32},{32,40},{40,48},{48,56},{56,64},{64,7... | collective-permute-start | bytes 110600 | tf_op jit(solution)/shard_map/ppermute | solution.py:18
  295.3 17.9 %copy-start.22 = (f32[32,32]{1,0:T(8,128)}, f32[32,32]{1,0:T(8,128)S(1)}, u32[]{:S(2)}) copy-start(f32[32,32]{1,0:T(8,128)S(1)} %fusion.103) | copy-start | bytes 12292
  295.3 7.8 %copy-start.11 = (bf16[2,192,48]{2,1,0:T(8,128)(2,1)}, bf16[2,192,48]{2,1,0:T(8,128)(2,1)S(1)}, u32[]{:S(2)}) copy-start(bf16[2,192,48]{2,1,0:T(8,128)(2,1)S(1)} %collective-permute-done.10) | copy-start | bytes 110596
  295.3 7.9 %collective-permute-start.11 = (bf16[2,192,48]{2,1,0:T(8,128)(2,1)S(1)}, bf16[2,192,48]{2,1,0:T(8,128)(2,1)}, u32[]{:S(2)}, u32[]{:S(2)}) collective-permute-start(bf16[2,192,48]{2,1,0:T(8,128)(2,1)S(1)} %collective-permute-done.10), channel_id=1, source_target_pairs={{0,120},{8,0},{16,8},{24,16},{32,24},{40,32},{48,40},{56,48},{64,5... | collective-permute-start | bytes 110600 | tf_op jit(solution)/shard_map/ppermute | solution.py:20
  303.1 10.1 %collective-permute-start.4 = (bf16[2,192,48]{2,1,0:T(8,128)(2,1)S(1)}, bf16[2,192,48]{2,1,0:T(8,128)(2,1)}, u32[]{:S(2)}, u32[]{:S(2)}) collective-permute-start(bf16[2,192,48]{2,1,0:T(8,128)(2,1)S(1)} %collective-permute-done.3), channel_id=1, source_target_pairs={{0,8},{8,16},{16,24},{24,32},{32,40},{40,48},{48,56},{56,64},{64,7... | collective-permute-start | bytes 110600 | tf_op jit(solution)/shard_map/ppermute | solution.py:18
  303.8 9.7 %collective-permute-start.12 = (bf16[2,192,48]{2,1,0:T(8,128)(2,1)}, bf16[2,192,48]{2,1,0:T(8,128)(2,1)}, u32[]{:S(2)}, u32[]{:S(2)}) collective-permute-start(bf16[2,192,48]{2,1,0:T(8,128)(2,1)} %collective-permute-done.11), channel_id=1, source_target_pairs={{0,120},{8,0},{16,8},{24,16},{32,24},{40,32},{48,40},{56,48},{64,5... | collective-permute-start | bytes 110600 | tf_op jit(solution)/shard_map/ppermute | solution.py:20
  313.2 9.3 %collective-permute-start.5 = (bf16[2,192,48]{2,1,0:T(8,128)(2,1)}, bf16[2,192,48]{2,1,0:T(8,128)(2,1)}, u32[]{:S(2)}, u32[]{:S(2)}) collective-permute-start(bf16[2,192,48]{2,1,0:T(8,128)(2,1)} %collective-permute-done.4), channel_id=1, source_target_pairs={{0,8},{8,16},{16,24},{24,32},{32,40},{40,48},{48,56},{56,64},{64,7... | collective-permute-start | bytes 110600 | tf_op jit(solution)/shard_map/ppermute | solution.py:18
  313.5 9.9 %collective-permute-start.13 = (bf16[2,192,48]{2,1,0:T(8,128)(2,1)}, bf16[2,192,48]{2,1,0:T(8,128)(2,1)}, u32[]{:S(2)}, u32[]{:S(2)}) collective-permute-start(bf16[2,192,48]{2,1,0:T(8,128)(2,1)} %collective-permute-done.12), channel_id=1, source_target_pairs={{0,120},{8,0},{16,8},{24,16},{32,24},{40,32},{48,40},{56,48},{64,5... | collective-permute-start | bytes 110600 | tf_op jit(solution)/shard_map/ppermute | solution.py:20
  322.5 8.3 %collective-permute-start.6 = (bf16[2,192,48]{2,1,0:T(8,128)(2,1)}, bf16[2,192,48]{2,1,0:T(8,128)(2,1)}, u32[]{:S(2)}, u32[]{:S(2)}) collective-permute-start(bf16[2,192,48]{2,1,0:T(8,128)(2,1)} %collective-permute-done.5), channel_id=1, source_target_pairs={{0,8},{8,16},{16,24},{24,32},{32,40},{40,48},{48,56},{56,64},{64,7... | collective-permute-start | bytes 110600 | tf_op jit(solution)/shard_map/ppermute | solution.py:18
  323.4 11.8 %collective-permute-start.14 = (bf16[2,192,48]{2,1,0:T(8,128)(2,1)}, bf16[2,192,48]{2,1,0:T(8,128)(2,1)}, u32[]{:S(2)}, u32[]{:S(2)}) collective-permute-start(bf16[2,192,48]{2,1,0:T(8,128)(2,1)} %collective-permute-done.13), channel_id=1, source_target_pairs={{0,120},{8,0},{16,8},{24,16},{32,24},{40,32},{48,40},{56,48},{64,5... | collective-permute-start | bytes 110600 | tf_op jit(solution)/shard_map/ppermute | solution.py:20
  330.8 8.3 %collective-permute-start.7 = (bf16[2,192,48]{2,1,0:T(8,128)(2,1)}, bf16[2,192,48]{2,1,0:T(8,128)(2,1)}, u32[]{:S(2)}, u32[]{:S(2)}) collective-permute-start(bf16[2,192,48]{2,1,0:T(8,128)(2,1)} %collective-permute-done.6), channel_id=1, source_target_pairs={{0,8},{8,16},{16,24},{24,32},{32,40},{40,48},{48,56},{56,64},{64,7... | collective-permute-start | bytes 110600 | tf_op jit(solution)/shard_map/ppermute | solution.py:18
  (23 other events, 77.7 us)
Sparse Core Ops, SparseCore 0:
  17.5 84.7 all-reduce.5
  132.0 123.2 all-reduce.7
  274.9 44.5 all-gather.1
